TPU v7x, 256 devices: a whole 4x4x8 slice. The times are simulated.
256 devices in a mesh: dp: 16 (over x, y), tensor: 16 (over z, core).
Axes of the slice: x: 4, y: 4, z: 8, core: 2. Of those that a mesh axis runs over, the one named last changes fastest.
Arguments:
- tokens: bfloat16 [1024, 8192], P('tensor', 'dp'), may hold values from -6 to 6
- grad_output: bfloat16 [1024, 8192], P('tensor', 'dp'), may hold values from -6 to 6
- gate_weight: bfloat16 [8192, 14336], P('dp', 'tensor'), may hold values from -0.09375 to 0.09375
- up_weight: bfloat16 [8192, 14336], P('dp', 'tensor'), may hold values from -0.09375 to 0.09375
- down_weight: bfloat16 [14336, 8192], P('tensor', 'dp'), may hold values from -0.0625 to 0.0625
- gate_mask: int32 [64, 112], P('dp', 'tensor'), may hold values 0 or 1
- up_mask: int32 [64, 112], P('dp', 'tensor'), may hold values 0 or 1
- down_mask: int32 [112, 64], P('tensor', 'dp'), may hold values 0 or 1
Outputs:
- output: bfloat16 [1024, 8192], P('tensor', 'dp')
- grad_tokens: bfloat16 [1024, 8192], P('tensor', 'dp')
- grad_gate: bfloat16 [8192, 14336], P('dp', 'tensor')
- grad_up: bfloat16 [8192, 14336], P('dp', 'tensor')
- grad_down: bfloat16 [14336, 8192], P('tensor', 'dp')
All inputs are finite; a program needn't handle non-finite values. No bound on the sum of `gate_mask` or of `up_mask` or of `down_mask` on one device may be relied on, other than what follows from the above.
Results may differ from a plain program's by a relative error of at most 0.005.
Values may be sent and summed in bfloat16 or wider, within the bound.
A program may use at most 128 MiB of HBM per device.

v0:
```python
import jax
import jax.numpy as jnp
from jax import lax
from jax.sharding import PartitionSpec as P


def spread(mask_table, weight):
    side = weight.shape[0] // mask_table.shape[0]
    return jnp.repeat(jnp.repeat(mask_table, side, axis=0), side, axis=1).astype(jnp.bfloat16)


def contract_rows(left, right_side):
    return lax.dot_general(
        left, right_side, (((0,), (0,)), ((), ())), preferred_element_type=jnp.float32
    )


def contract_cols(left, right_side):
    return lax.dot_general(
        left, right_side, (((1,), (1,)), ((), ())), preferred_element_type=jnp.float32
    )


def shards(tokens, grad_output, gate_weight, up_weight, down_weight, gate_mask, up_mask, down_mask):
    gate_keep = spread(gate_mask, gate_weight)
    up_keep = spread(up_mask, up_weight)
    down_keep = spread(down_mask, down_weight)
    gate_eff = gate_weight * gate_keep
    up_eff = up_weight * up_keep
    down_eff = down_weight * down_keep
    rows_all, cotangents = (
        lax.all_gather(tokens, "tensor", axis=0, tiled=True),
        lax.all_gather(grad_output, "tensor", axis=0, tiled=True),
    )
    part_gate = jnp.dot(rows_all, gate_eff, preferred_element_type=jnp.float32)
    part_up = jnp.dot(rows_all, up_eff, preferred_element_type=jnp.float32)
    share_rows = rows_all.shape[0] // lax.axis_size("dp")
    gate_full, up_full = lax.psum((part_gate, part_up), "dp")
    hidden_all = (gate_full * jax.nn.sigmoid(gate_full) * up_full).astype(jnp.bfloat16)
    first_row = lax.axis_index("dp") * share_rows
    gate_own = lax.dynamic_slice_in_dim(gate_full, first_row, share_rows, 0)
    up_own = lax.dynamic_slice_in_dim(up_full, first_row, share_rows, 0)
    output = lax.psum_scatter(
        jnp.dot(hidden_all, down_eff, preferred_element_type=jnp.float32),
        "tensor",
        scatter_dimension=0,
        tiled=True,
    ).astype(jnp.bfloat16)
    grad_down = (down_keep.astype(jnp.float32) * contract_rows(hidden_all, cotangents)).astype(
        jnp.bfloat16
    )
    part_hidden = contract_cols(cotangents, down_eff)
    grad_hidden = lax.psum_scatter(part_hidden, "dp", scatter_dimension=0, tiled=True)
    sigmoid_gate = jax.nn.sigmoid(gate_own)
    activated = gate_own * sigmoid_gate
    grad_gate_act = (
        grad_hidden * up_own * sigmoid_gate * (1.0 + gate_own * (1.0 - sigmoid_gate))
    ).astype(jnp.bfloat16)
    grad_up_act = (grad_hidden * activated).astype(jnp.bfloat16)
    gate_grads_all, up_grads_all = (
        lax.all_gather(grad_gate_act, "dp", axis=0, tiled=True),
        lax.all_gather(grad_up_act, "dp", axis=0, tiled=True),
    )
    grad_gate = (gate_keep.astype(jnp.float32) * contract_rows(rows_all, gate_grads_all)).astype(
        jnp.bfloat16
    )
    grad_up = (up_keep.astype(jnp.float32) * contract_rows(rows_all, up_grads_all)).astype(
        jnp.bfloat16
    )
    grad_tokens = lax.psum_scatter(
        contract_cols(gate_grads_all, gate_eff) + contract_cols(up_grads_all, up_eff),
        "tensor",
        scatter_dimension=0,
        tiled=True,
    ).astype(jnp.bfloat16)
    return (output, grad_tokens, grad_gate, grad_up, grad_down)


def solution(mesh):
    return jax.shard_map(
        shards,
        mesh=mesh,
        in_specs=(
            P("tensor", "dp"),
            P("tensor", "dp"),
            P("dp", "tensor"),
            P("dp", "tensor"),
            P("tensor", "dp"),
            P("dp", "tensor"),
            P("dp", "tensor"),
            P("tensor", "dp"),
        ),
        out_specs=(
            P("tensor", "dp"),
            P("tensor", "dp"),
            P("dp", "tensor"),
            P("dp", "tensor"),
            P("tensor", "dp"),
        ),
        check_vma=False,
    )
```

profile of v0, /device:TPU:2, one launch (start us, length us, event | category | flops | bytes accessed | tf_op | source)
XLA Modules:
  0.0 554.3 jit_solution(4922906366583342277)
XLA Ops:
  7.2 0.7 all-gather.5.cloned.1.call-update
  8.0 0.7 all-gather.7.cloned.1.call-update
  8.7 0.7 convert_element_type.69
  9.4 0.1 copy.32
  9.5 0.1 broadcast_bitcast_fusion
  9.6 1.5 copy.33
  11.1 0.1 copy.29
  11.2 0.1 broadcast_bitcast_fusion.1
  11.3 0.5 copy.30
  11.8 0.1 bitcast_multiply_fusion.2
  11.9 0.1 bitcast_multiply_fusion.3
  12.0 39.4 %all-gather.5.cloned.1.call-done = bf16[1024,512]{1,0:T(8,128)(2,1)} async-done(((bf16[64,512]{1,0:T(8,128)(2,1)}), bf16[1024,512]{1,0:T(8,128)(2,1)}) %all-gather.5.cloned.1.call-update) | async-done | bytes 1048592 | tf_op jit(solution)/shard_map/all_gather | solution.py:32
  51.4 4.5 convolution_bitcast_fusion.1
  55.9 3.2 convolution_bitcast_fusion.2
  59.1 0.0 reduce-scatter.10.cloned.1.call-start
  59.2 0.6 copy-done.9
  59.8 0.1 copy.35
  59.9 30.6 %all-gather.7.cloned.1.call-done = bf16[1024,512]{1,0:T(8,128)(2,1)} async-done(((bf16[64,512]{1,0:T(8,128)(2,1)}), bf16[1024,512]{1,0:T(8,128)(2,1)}) %all-gather.7.cloned.1.call-update) | async-done | bytes 1048592 | tf_op jit(solution)/shard_map/all_gather | solution.py:33
  90.6 1.1 broadcast_in_dim.23
  91.7 0.9 copy-done.1
  92.6 4.2 convolution_bitcast_fusion
  96.8 5.1 copy.42
  101.9 0.0 all-gather.9.cloned.1.call-start
  102.0 132.5 %all-reduce.3.cloned.1.call-done = (f32[1024,896]{1,0:T(8,128)}, f32[1024,896]{1,0:T(8,128)}) async-done(((f32[1024,896]{1,0:T(8,128)}, f32[1024,896]{1,0:T(8,128)}), (f32[1024,896]{1,0:T(8,128)}, f32[1024,896]{1,0:T(8,128)})) %all-reduce.3.cloned.1.call-update) | async-done | bytes 7340048 | tf_op jit(solution)/shard_map/psum | solution.py:38
  234.5 85.1 %reduce-scatter.10.cloned.1.call-done = f32[64,896]{1,0:T(8,128)} async-done(((f32[1024,896]{1,0:T(8,128)}), f32[64,896]{1,0:T(8,128)}) %reduce-scatter.10.cloned.1.call-update) | async-done | bytes 229392 | tf_op jit(solution)/shard_map/reduce_scatter | solution.py:53
  319.6 2.0 multiply_convert_fusion.2
  321.6 0.0 all-gather.11.cloned.1.call-start
  321.7 0.5 all-gather.11.cloned.1.call-update
  322.3 4.3 multiply_convert_fusion
  326.5 1.2 copy-done.4
  327.8 2.6 fusion.2
  330.4 0.0 reduce-scatter.8.cloned.1.call-start
  330.4 41.2 %all-gather.9.cloned.1.call-done = bf16[1024,896]{1,0:T(8,128)(2,1)} async-done(((bf16[64,896]{1,0:T(8,128)(2,1)}), bf16[1024,896]{1,0:T(8,128)(2,1)}) %all-gather.9.cloned.1.call-update) | async-done | bytes 1835024 | tf_op jit(solution)/shard_map/all_gather | solution.py:61
  371.6 4.0 fusion.3
  375.6 48.0 %all-gather.11.cloned.1.call-done = bf16[1024,896]{1,0:T(8,128)(2,1)} async-done(((bf16[64,896]{1,0:T(8,128)(2,1)}), bf16[1024,896]{1,0:T(8,128)(2,1)}) %all-gather.11.cloned.1.call-update) | async-done | bytes 1835024 | tf_op jit(solution)/shard_map/all_gather | solution.py:62
  423.6 4.7 convolution_add_fusion
  428.4 1.2 copy-done.3
  429.5 4.0 multiply_convert_fusion.1
  433.5 0.1 broadcast_in_dim.19
  433.6 1.2 fusion.1
  434.7 1.3 copy.38
  436.0 0.1 broadcast_in_dim.21
  436.1 2.7 fusion
  438.8 1.3 copy.39
  440.0 45.4 %reduce-scatter.6.cloned.1.call-done = f32[64,512]{1,0:T(8,128)} async-done(((f32[1024,512]{1,0:T(8,128)}), f32[64,512]{1,0:T(8,128)}) %reduce-scatter.6.cloned.1.call-update) | async-done | bytes 131088 | tf_op jit(solution)/shard_map/reduce_scatter | solution.py:43
  485.4 1.5 convert_element_type.76
  487.0 59.0 %reduce-scatter.8.cloned.1.call-done = f32[64,512]{1,0:T(8,128)} async-done(((f32[1024,512]{1,0:T(8,128)}), f32[64,512]{1,0:T(8,128)}) %reduce-scatter.8.cloned.1.call-update) | async-done | bytes 131088 | tf_op jit(solution)/shard_map/reduce_scatter | solution.py:70
  545.9 1.5 convert_element_type.79
  (32 shorter events, 0.3 us)
Async XLA Ops:
  7.2 3.9 copy-start.8
  7.2 4.1 copy-start.7
  7.2 44.2 %all-gather.5.cloned.1.call-start = ((), (), s32[]{:S(2)}) async-start(), calls=%async_computation.3 | async-start | bytes 1114112 | tf_op jit(solution)/shard_map/all_gather | solution.py:32
  7.9 82.6 %all-gather.7.cloned.1.call-start = ((), (), s32[]{:S(2)}) async-start(), calls=%async_computation.5 | async-start | bytes 1114112 | tf_op jit(solution)/shard_map/all_gather | solution.py:33
  8.7 225.8 %all-reduce.3.cloned.1.call-start = ((), (), s32[]{:S(2)}) async-start(), calls=%async_computation.10 | async-start | bytes 14680064 | tf_op jit(solution)/shard_map/psum | solution.py:38
  51.4 4.5 copy-start
  59.1 0.7 copy-start.9
  59.1 260.5 %reduce-scatter.10.cloned.1.call-start = ((), (), s32[]{:S(2)}) async-start(), calls=%async_computation.9 | async-start | bytes 3899392 | tf_op jit(solution)/shard_map/reduce_scatter | solution.py:53
  90.5 2.1 copy-start.5
  91.7 0.9 copy-start.1
  101.9 269.7 %all-gather.9.cloned.1.call-start = ((), (), s32[]{:S(2)}) async-start(), calls=%async_computation.6 | async-start | bytes 1949696 | tf_op jit(solution)/shard_map/all_gather | solution.py:61
  321.6 102.0 %all-gather.11.cloned.1.call-start = ((), (), s32[]{:S(2)}) async-start(), calls=%async_computation.7 | async-start | bytes 1949696 | tf_op jit(solution)/shard_map/all_gather | solution.py:62
  322.2 163.2 %reduce-scatter.6.cloned.1.call-start = ((), (), s32[]{:S(2)}) async-start(), calls=%async_computation.4 | async-start | bytes 2228224 | tf_op jit(solution)/shard_map/reduce_scatter | solution.py:43
  322.2 5.5 %copy-start.2 = (bf16[896,4,128]{2,1,0:T(4,128)(2,1)S(1)}, bf16[896,4,128]{2,1,0:T(4,128)(2,1)}, u32[]{:S(2)}) copy-start(bf16[896,4,128]{2,1,0:T(4,128)(2,1)} %copy-done.1) | copy-start | bytes 2752516
  322.2 5.5 copy-start.6
  326.5 1.3 copy-start.4
  330.4 215.5 %reduce-scatter.8.cloned.1.call-start = ((), (), s32[]{:S(2)}) async-start(), calls=%async_computation.8 | async-start | bytes 2228224 | tf_op jit(solution)/shard_map/reduce_scatter | solution.py:70
  428.3 1.2 copy-start.3
  429.5 4.1 copy-start.10
Sparse Core Ops, SparseCore 0:
  9.8 41.5 all-gather.4
  53.2 37.2 all-gather.6
  94.0 140.4 all-reduce.2
  238.5 81.1 reduce-scatter.9
  322.8 48.7 all-gather.8
  374.8 48.7 all-gather.10
  426.3 59.0 reduce-scatter.5
  488.1 57.7 reduce-scatter.7
where the time goes:
time: 555 us; the launch traced here: 554 us
  waiting for transfers between devices  483 us (87%)
  matrix products  31.1 us (6%)
  local copies, waits for them, and re-layouts  15.3 us (3%)
  between operations  14.3 us (3%)
  other arithmetic  10.1 us (2%)
    psum x1, waiting for transfers between devices, shards(): gate_full, up_full = lax.psum((part_gate, part_up), 'dp')  133 us
    reduce_scatter x1, waiting for transfers between devices, shards(): lax.psum_scatter(part_hidden, 'dp', scatter_dimension=0, tiled=True)  85.1 us
    reduce_scatter x1, waiting for transfers between devices, shards(): lax.psum_scatter(contract_cols(gate_grads_all, gate_eff) + contract_cols(...  59 us
    all_gather x1, waiting for transfers between devices, shards(): lax.all_gather(grad_up_act, 'dp', axis=0, tiled=True)  48 us
    reduce_scatter x1, waiting for transfers between devices, shards(): lax.psum_scatter(jnp.dot(hidden_all, down_eff, preferred_element_type=jnp...  45.4 us
    all_gather x1, waiting for transfers between devices, shards(): lax.all_gather(grad_gate_act, 'dp', axis=0, tiled=True)  41.2 us
    all_gather x1, waiting for transfers between devices, shards(): lax.all_gather(tokens, 'tensor', axis=0, tiled=True)  39.4 us
    all_gather x1, waiting for transfers between devices, shards(): lax.all_gather(grad_output, 'tensor', axis=0, tiled=True)  30.6 us
  transfers between devices with their start and end apart: 8, of which 8 were waited for; matrix products, arithmetic and copies ran while one was open for 9% of the time, Pallas kernels for 0%

commit v1 on v0

--- a/solution.py
+++ b/solution.py
@@ -58,7 +58,9 @@
     ).astype(jnp.bfloat16)
     grad_up_act = (grad_hidden * activated).astype(jnp.bfloat16)
     gate_grads_all, up_grads_all = (
-        lax.all_gather(grad_gate_act, "dp", axis=0, tiled=True),
+        jnp.concatenate(
+            lax.all_to_all(jnp.stack([grad_gate_act] * lax.axis_size("dp")), "dp", 0, 0), axis=0
+        ),
         lax.all_gather(grad_up_act, "dp", axis=0, tiled=True),
     )
     grad_gate = (gate_keep.astype(jnp.float32) * contract_rows(rows_all, gate_grads_all)).astype(

time: 555 us -> 513 us (0.924)
  waiting for transfers between devices: 483 us -> 412 us
  blocking collectives: 0 us -> 29.4 us
    all_gather x1 -> x0, waiting for transfers between devices: 41.2 us -> none  [shards(): lax.all_gather(grad_gate_act, 'dp', axis=0, tiled=True)]
    all_gather x1, waiting for transfers between devices: 48 us -> 18.3 us  [shards(): lax.all_gather(grad_up_act, 'dp', axis=0, tiled=True)]
    all_to_all x0 -> x1, blocking collectives: none -> 29.4 us  [shards(): lax.all_to_all(jnp.stack([grad_gate_act] * lax.axis_size('dp')), 'dp', 0, 0)]
    unnamed x31 -> x33, local copies, waits for them, and re-layouts: 13.7 us -> 14.9 us
  transfers between devices with their start and end apart: 8 -> 7, of which waited for: 8 -> 7; matrix products, arithmetic and copies ran while one was open for 9% -> 9% of each run, Pallas kernels for 0% -> 0%
where the time goes in v1:
time: 513 us; the launch traced here: 512 us
  waiting for transfers between devices  412 us (80%)
  matrix products  29.7 us (6%)
  blocking collectives  29.4 us (6%)
  local copies, waits for them, and re-layouts  16.8 us (3%)
  between operations  14.3 us (3%)
  other arithmetic  10.1 us (2%)
    psum x1, waiting for transfers between devices, shards(): gate_full, up_full = lax.psum((part_gate, part_up), 'dp')  133 us
    reduce_scatter x1, waiting for transfers between devices, shards(): lax.psum_scatter(part_hidden, 'dp', scatter_dimension=0, tiled=True)  85.1 us
    reduce_scatter x1, waiting for transfers between devices, shards(): lax.psum_scatter(contract_cols(gate_grads_all, gate_eff) + contract_cols(...  59 us
    reduce_scatter x1, waiting for transfers between devices, shards(): lax.psum_scatter(jnp.dot(hidden_all, down_eff, preferred_element_type=jnp...  45.2 us
    all_gather x1, waiting for transfers between devices, shards(): lax.all_gather(tokens, 'tensor', axis=0, tiled=True)  39.4 us
    all_gather x1, waiting for transfers between devices, shards(): lax.all_gather(grad_output, 'tensor', axis=0, tiled=True)  30.6 us
    all_to_all x1, blocking collectives, shards(): lax.all_to_all(jnp.stack([grad_gate_act] * lax.axis_size('dp')), 'dp', 0, 0)  29.4 us
    all_gather x1, waiting for transfers between devices, shards(): lax.all_gather(grad_up_act, 'dp', axis=0, tiled=True)  18.3 us
  transfers between devices with their start and end apart: 7, of which 7 were waited for; matrix products, arithmetic and copies ran while one was open for 9% of the time, Pallas kernels for 0%

profile of v1, /device:TPU:2, one launch (start us, length us, event | category | flops | bytes accessed | tf_op | source)
XLA Modules:
  0.0 512.1 jit_solution(15849986199540769162)
XLA Ops:
  7.2 0.7 all-gather.4.cloned.1.call-update
  8.0 0.7 all-gather.6.cloned.1.call-update
  8.7 0.7 convert_element_type.69
  9.4 0.1 copy.33
  9.5 0.1 broadcast_bitcast_fusion
  9.6 1.5 copy.34
  11.1 0.1 copy.30
  11.2 0.1 broadcast_bitcast_fusion.1
  11.3 0.5 copy.31
  11.8 0.1 bitcast_multiply_fusion.2
  11.9 0.1 bitcast_multiply_fusion.3
  12.0 39.4 %all-gather.4.cloned.1.call-done = bf16[1024,512]{1,0:T(8,128)(2,1)} async-done(((bf16[64,512]{1,0:T(8,128)(2,1)}), bf16[1024,512]{1,0:T(8,128)(2,1)}) %all-gather.4.cloned.1.call-update) | async-done | bytes 1048592 | tf_op jit(solution)/shard_map/all_gather | solution.py:32
  51.4 4.5 convolution_bitcast_fusion.1
  55.9 3.2 convolution_bitcast_fusion.2
  59.1 0.0 reduce-scatter.10.cloned.1.call-start
  59.2 0.6 copy-done.11
  59.8 0.1 copy.36
  59.9 30.6 %all-gather.6.cloned.1.call-done = bf16[1024,512]{1,0:T(8,128)(2,1)} async-done(((bf16[64,512]{1,0:T(8,128)(2,1)}), bf16[1024,512]{1,0:T(8,128)(2,1)}) %all-gather.6.cloned.1.call-update) | async-done | bytes 1048592 | tf_op jit(solution)/shard_map/all_gather | solution.py:33
  90.6 1.1 broadcast_in_dim.23
  91.7 0.9 copy-done.1
  92.6 4.2 convolution_bitcast_fusion
  96.8 5.0 copy.43
  101.9 0.0 all-gather.8.cloned.1.call-start
  102.0 132.5 %all-reduce.3.cloned.1.call-done = (f32[1024,896]{1,0:T(8,128)}, f32[1024,896]{1,0:T(8,128)}) async-done(((f32[1024,896]{1,0:T(8,128)}, f32[1024,896]{1,0:T(8,128)}), (f32[1024,896]{1,0:T(8,128)}, f32[1024,896]{1,0:T(8,128)})) %all-reduce.3.cloned.1.call-update) | async-done | bytes 7340048 | tf_op jit(solution)/shard_map/psum | solution.py:38
  234.5 85.1 %reduce-scatter.10.cloned.1.call-done = f32[64,896]{1,0:T(8,128)} async-done(((f32[1024,896]{1,0:T(8,128)}), f32[64,896]{1,0:T(8,128)}) %reduce-scatter.10.cloned.1.call-update) | async-done | bytes 229392 | tf_op jit(solution)/shard_map/reduce_scatter | solution.py:53
  319.6 1.9 multiply_convert_fusion.2
  321.5 0.0 reduce-scatter.6.cloned.1.call-start
  321.6 4.3 multiply_convert_fusion
  325.9 1.2 copy-done.6
  327.1 2.6 fusion.2
  329.8 0.2 stack.2
  330.1 29.4 %all_to_all.5 = bf16[16,64,896]{2,1,0:T(8,128)(2,1)S(1)} all-to-all(bf16[16,64,896]{2,1,0:T(8,128)(2,1)S(1)} %stack.2), channel_id=1, replica_groups=mesh['dp'=16,'tensor'=16] {'dp'}, dimensions={0} | all-to-all | bytes 3670016 | tf_op jit(solution)/shard_map/all_to_all | solution.py:62
  359.5 1.2 copy-done.4
  360.7 2.6 fusion.3
  363.3 18.3 %all-gather.8.cloned.1.call-done = bf16[1024,896]{1,0:T(8,128)(2,1)} async-done(((bf16[64,896]{1,0:T(8,128)(2,1)}), bf16[1024,896]{1,0:T(8,128)(2,1)}) %all-gather.8.cloned.1.call-update) | async-done | bytes 1835024 | tf_op jit(solution)/shard_map/all_gather | solution.py:64
  381.6 4.7 convolution_add_fusion
  386.3 1.2 copy-done.3
  387.5 4.0 multiply_convert_fusion.1
  391.4 0.1 broadcast_in_dim.19
  391.5 1.2 fusion.1
  392.7 1.3 copy.39
  394.0 0.1 broadcast_in_dim.21
  394.0 2.7 fusion
  396.8 1.3 copy.40
  398.0 45.2 %reduce-scatter.6.cloned.1.call-done = f32[64,512]{1,0:T(8,128)} async-done(((f32[1024,512]{1,0:T(8,128)}), f32[64,512]{1,0:T(8,128)}) %reduce-scatter.6.cloned.1.call-update) | async-done | bytes 131088 | tf_op jit(solution)/shard_map/reduce_scatter | solution.py:43
  443.2 1.5 convert_element_type.76
  444.8 59.0 %reduce-scatter.8.cloned.1.call-done = f32[64,512]{1,0:T(8,128)} async-done(((f32[1024,512]{1,0:T(8,128)}), f32[64,512]{1,0:T(8,128)}) %reduce-scatter.8.cloned.1.call-update) | async-done | bytes 131088 | tf_op jit(solution)/shard_map/reduce_scatter | solution.py:72
  503.7 1.5 convert_element_type.79
  (33 shorter events, 0.3 us)
Async XLA Ops:
  7.2 3.9 copy-start.10
  7.2 4.1 copy-start.9
  7.2 44.2 %all-gather.4.cloned.1.call-start = ((), (), s32[]{:S(2)}) async-start(), calls=%async_computation.4 | async-start | bytes 1114112 | tf_op jit(solution)/shard_map/all_gather | solution.py:32
  7.9 82.6 %all-gather.6.cloned.1.call-start = ((), (), s32[]{:S(2)}) async-start(), calls=%async_computation.6 | async-start | bytes 1114112 | tf_op jit(solution)/shard_map/all_gather | solution.py:33
  8.7 225.8 %all-reduce.3.cloned.1.call-start = ((), (), s32[]{:S(2)}) async-start(), calls=%async_computation.10 | async-start | bytes 14680064 | tf_op jit(solution)/shard_map/psum | solution.py:38
  51.4 4.5 copy-start
  59.1 0.7 copy-start.11
  59.1 260.4 %reduce-scatter.10.cloned.1.call-start = ((), (), s32[]{:S(2)}) async-start(), calls=%async_computation.9 | async-start | bytes 3899392 | tf_op jit(solution)/shard_map/reduce_scatter | solution.py:53
  90.5 2.1 copy-start.7
  91.7 0.9 copy-start.1
  101.9 279.7 %all-gather.8.cloned.1.call-start = ((), (), s32[]{:S(2)}) async-start(), calls=%async_computation.7 | async-start | bytes 1949696 | tf_op jit(solution)/shard_map/all_gather | solution.py:64
  321.5 121.7 %reduce-scatter.6.cloned.1.call-start = ((), (), s32[]{:S(2)}) async-start(), calls=%async_computation.5 | async-start | bytes 2228224 | tf_op jit(solution)/shard_map/reduce_scatter | solution.py:43
  321.6 5.5 %copy-start.2 = (bf16[896,4,128]{2,1,0:T(4,128)(2,1)S(1)}, bf16[896,4,128]{2,1,0:T(4,128)(2,1)}, u32[]{:S(2)}) copy-start(bf16[896,4,128]{2,1,0:T(4,128)(2,1)} %copy-done.1) | copy-start | bytes 2752516
  321.6 5.5 %copy-start.8 = (bf16[896,512]{1,0:T(8,128)(2,1)S(1)}, bf16[896,512]{1,0:T(8,128)(2,1)}, u32[]{:S(2)}) copy-start(bf16[896,512]{1,0:T(8,128)(2,1)} %param.12) | copy-start | bytes 2752516
  325.9 1.2 copy-start.6
  329.8 174.0 %reduce-scatter.8.cloned.1.call-start = ((), (), s32[]{:S(2)}) async-start(), calls=%async_computation.8 | async-start | bytes 2228224 | tf_op jit(solution)/shard_map/reduce_scatter | solution.py:72
  359.5 1.2 copy-start.4
  386.3 1.2 copy-start.3
  387.5 4.1 copy-start.5
Sparse Core Ops, SparseCore 0:
  9.8 41.5 all-gather.3
  53.2 37.2 all-gather.5
  94.0 140.4 all-reduce.2
  238.4 81.1 reduce-scatter.9
  322.8 58.7 all-gather.7
  384.1 59.0 reduce-scatter.5
  445.9 57.7 reduce-scatter.7
